TPU v7x, 32 devices: a whole 2x2x4 slice. The times are simulated.
32 devices in a mesh: rows: 16 (over z, y, x), feat: 2 (over core).
Axes of the slice: x: 2, y: 2, z: 4, core: 2. Of those that a mesh axis runs over, the one named last changes fastest.
Arguments:
- embeddings: bfloat16 [12288, 768], P('rows', 'feat'), may hold values from -6 to 6
- factor: float32 [12288, 256], P(('rows', 'feat')), may hold values from -0.1 to 0.1, as said below
- residual_diag: float32 [12288], P(('rows', 'feat')), may hold values from 0.5 to 1.5
- pivots: int32 [2, 256], replicated, may hold values from 0 to 12287, as said below
Outputs:
- new_columns: float32 [2, 12288, 256], P(None, ('rows', 'feat'))
- residual_out: float32 [12288], P(('rows', 'feat'))
Inputs may be any that keep to these rules, and one draw needn't show every extreme that they name: Each block's 256 pivots are distinct and increasing, the two blocks share none, and in each block at most 32 pivots lie among the 768 candidates of one index of rows; some index holds exactly 32 in every block. `factor`: entries are independent.
All inputs are finite; a program needn't handle non-finite values.
Results may differ from a plain program's by a relative error of at most 0.0003.
Values may be sent and summed in bfloat16 or wider, within the bound.
No kernel may reach another device: no remote copies, remote signals or barrier semaphores. Data moves between devices by JAX's collectives and lax.ppermute only.
A program may use at most 64 MiB of HBM per device.

v0:
```python
import jax
import jax.numpy as jnp
from jax import lax
from jax.sharding import PartitionSpec as P

ridge_weight = 2.0


def shards(embeddings, factor, residual_diag, pivots):
    local_rows = embeddings.shape[0]
    half_rows = factor.shape[0]
    feat_cols = embeddings.shape[1]
    feat_count = lax.axis_size("feat")
    full_width = feat_cols * feat_count
    row_group = lax.axis_index("rows")
    feat_group = lax.axis_index("feat")
    rows_start = row_group * local_rows
    half_start = rows_start + feat_group * half_rows
    global_ids = half_start + jnp.arange(half_rows, dtype=jnp.int32)
    partial_norms = jnp.sum(jnp.square(embeddings.astype(jnp.float32)), axis=1)
    row_norms = partial_norms
    current = factor
    fresh_list = []
    for block_id in range(2):
        chosen_ids = pivots[block_id]
        pivot_count = chosen_ids.shape[0]
        offsets = chosen_ids - rows_start
        owned_mask = (offsets >= 0) & (offsets < local_rows)
        safe_rows = jnp.clip(offsets, 0, local_rows - 1)
        half_offsets = offsets - feat_group * half_rows
        half_mask = owned_mask & (half_offsets >= 0) & (half_offsets < half_rows)
        half_safe = jnp.clip(half_offsets, 0, half_rows - 1)
        capacity = max(2, 2 * pivot_count // lax.axis_size("rows"))
        owners = chosen_ids // local_rows
        earlier = jnp.sum((owners[None, :] < owners[:, None]).astype(jnp.int32), axis=1)
        pivot_ranks = jnp.arange(pivot_count, dtype=jnp.int32) - earlier
        slot_hits = (
            pivot_ranks[None, :] == jnp.arange(capacity, dtype=jnp.int32)[:, None]
        ) & owned_mask[None, :]
        slot_full = jnp.any(slot_hits, axis=1)
        slot_rows = jnp.sum(jnp.where(slot_hits, safe_rows[None, :], 0), axis=1)
        half_hits = slot_hits & half_mask[None, :]
        slot_half = jnp.any(half_hits, axis=1)
        slot_half_rows = jnp.sum(jnp.where(half_hits, half_safe[None, :], 0), axis=1)
        packed_x = jnp.where(slot_full[:, None], jnp.take(embeddings, slot_rows, axis=0), 0)
        packed_f = jnp.where(slot_half[:, None], jnp.take(current, slot_half_rows, axis=0), 0.0)
        all_x = lax.all_gather(packed_x, ("rows", "feat"), axis=0, tiled=True)
        all_f = lax.all_gather(packed_f, ("rows", "feat"), axis=0, tiled=True)
        first_src = owners * feat_count * capacity + pivot_ranks
        pieces = []
        pivot_factor = jnp.zeros((pivot_count, current.shape[1]), jnp.float32)
        for feat_id in range(feat_count):
            source = first_src + feat_id * capacity
            pieces.append(jnp.take(all_x, source, axis=0))
            pivot_factor = pivot_factor + jnp.take(all_f, source, axis=0)
        chosen = jnp.concatenate(pieces, axis=1)
        own_cols = lax.dynamic_slice_in_dim(chosen, feat_group * feat_cols, feat_cols, 1)
        dots_part = jnp.einsum(
            "nd,kd->nk", embeddings, own_cols, preferred_element_type=jnp.float32
        )
        partial_terms = (dots_part, partial_norms) if block_id == 0 else (dots_part,)
        summed = lax.psum_scatter(partial_terms, "feat", scatter_dimension=0, tiled=True)
        dot_panel = summed[0]
        if block_id == 0:
            row_norms = summed[1]
        chosen_wide = chosen.astype(jnp.float32)
        chosen_norms = jnp.sum(chosen_wide * chosen_wide, axis=1)
        kernel_panel = jnp.exp(
            -(row_norms[:, None] + chosen_norms[None, :] - 2.0 * dot_panel) / (2.0 * full_width)
        )
        kernel_panel = kernel_panel + ridge_weight * (
            global_ids[:, None] == chosen_ids[None, :]
        ).astype(jnp.float32)
        kernel_panel = kernel_panel - jnp.dot(
            current,
            pivot_factor.T,
            precision=lax.Precision.HIGHEST,
            preferred_element_type=jnp.float32,
        )
        pivot_dots = jnp.einsum("kd,jd->kj", chosen, chosen, preferred_element_type=jnp.float32)
        pivot_block = jnp.exp(
            -(chosen_norms[:, None] + chosen_norms[None, :] - 2.0 * pivot_dots) / (2.0 * full_width)
        )
        pivot_block = pivot_block + ridge_weight * jnp.eye(pivot_count, dtype=jnp.float32)
        pivot_block = pivot_block - jnp.dot(
            pivot_factor,
            pivot_factor.T,
            precision=lax.Precision.HIGHEST,
            preferred_element_type=jnp.float32,
        )
        chol_lower = jnp.linalg.cholesky(pivot_block)
        fresh_cols = jax.scipy.linalg.solve_triangular(chol_lower, kernel_panel.T, lower=True).T
        fresh_list.append(fresh_cols)
        current = jnp.concatenate([current, fresh_cols], axis=1)
    removed = jnp.sum(fresh_list[0] * fresh_list[0], axis=1) + jnp.sum(
        fresh_list[1] * fresh_list[1], axis=1
    )
    return (jnp.stack(fresh_list), residual_diag - removed)


def solution(mesh):
    return jax.shard_map(
        shards,
        mesh=mesh,
        in_specs=(P("rows", "feat"), P(("rows", "feat"), None), P(("rows", "feat")), P()),
        out_specs=(P(None, ("rows", "feat"), None), P(("rows", "feat"))),
        check_vma=False,
    )
```

profile of v0, /device:TPU:0, one launch (start us, length us, event | category | flops | bytes accessed | tf_op | source)
XLA Modules:
  0.0 285.8 jit_solution(14113380142749730828)
XLA Ops:
  10.1 1.6 gather_fusion
  12.5 1.8 gather_fusion.2
  14.4 45.6 %all_gather.12 = bf16[1024,384]{1,0:T(8,128)(2,1)S(1)} all-gather(bf16[32,384]{1,0:T(8,128)(2,1)S(1)} %select_select_fusion.5), channel_id=1, replica_groups=mesh['rows'=16,'feat'=2] {'rows','feat'}, dimensions={0}, use_global_device_ids=true | all-gather | bytes 811008 | tf_op jit(solution)/shard_map/all_gather | solution.py:47
  62.6 1.3 convolution_bitcast_fusion.1
  67.5 2.8 all-reduce.1
  72.3 2.3 gather_fusion.5
  76.3 11.7 %cholesky.130 = f32[128,128]{1,0:T(8,128)S(1)} custom-call(f32[128,128]{1,0:T(8,128)S(1)} %cholesky.194), custom_call_target="Cholesky" | custom-call | tf_op jit(solution)/shard_map/jit(cholesky)/cholesky | solution.py:91
  88.1 9.8 %custom-call.13 = f32[1,128,128]{1,2,0:T(8,128)S(1)} custom-call(f32[1,128,128]{2,1,0:T(8,128)S(1)} %get-tuple-element.79), custom_call_target="InvertDiagBlocksLowerTriangular" | custom-call | tf_op jit(solution)/shard_map/jit(cholesky)/cholesky | solution.py:91
  98.4 11.7 %cholesky.147 = f32[128,128]{1,0:T(8,128)S(1)} custom-call(f32[128,128]{1,0:T(8,128)S(1)} %convolution_subtract_fusion.6), custom_call_target="Cholesky" | custom-call | tf_op jit(solution)/shard_map/jit(cholesky)/cholesky | solution.py:91
  112.9 15.5 %while.4 = (s32[]{:T(128)}, f32[256,256]{1,0:T(8,128)S(1)}, s32[2,2]{1,0:T(2,128)S(1)}, f32[2,128,128]{2,1,0:T(8,128)S(1)}, s32[]{:T(128)}) while((s32[]{:T(128)}, f32[256,256]{1,0:T(8,128)S(1)}, s32[2,2]{1,0:T(2,128)S(1)}, f32[2,128,128]{2,1,0:T(8,128)S(1)}, s32[]{:T(128)}) %tuple.77), condition=%wide.while_cond, body=%wide.while_body.sunk | while | flops 2 | bytes 131181 | solution.py:92
  125.1 1.4 bitcast_dynamic-update-slice_fusion.4
  127.0 1.4 bitcast_dynamic-update-slice_fusion.4
  128.4 19.7 %custom-call.14 = f32[2,128,128]{1,2,0:T(8,128)S(1)} custom-call(f32[2,128,128]{2,1,0:T(8,128)S(1)} %get-tuple-element.22), custom_call_target="InvertDiagBlocksLowerTriangular" | custom-call | tf_op jit(solution)/shard_map/jit(_solve_triangular)/triangular_solve | solution.py:92
  148.2 1.7 fusion.2
  154.5 39.7 %all_gather.14 = bf16[1024,384]{1,0:T(8,128)(2,1)S(1)} all-gather(bf16[32,384]{1,0:T(8,128)(2,1)S(1)} %select_select_fusion.4), channel_id=1, replica_groups=mesh['rows'=16,'feat'=2] {'rows','feat'}, dimensions={0}, use_global_device_ids=true | all-gather | bytes 811008 | tf_op jit(solution)/shard_map/all_gather | solution.py:47
  199.9 7.0 %all-gather.5.cloned.1.call-done = f32[1024,512]{1,0:T(8,128)} async-done(((f32[32,512]{1,0:T(8,128)}), f32[1024,512]{1,0:T(8,128)}) %all-gather.5.cloned.1.call-update) | async-done | bytes 2097168 | tf_op jit(solution)/shard_map/all_gather | solution.py:48
  206.9 2.9 %gather_fusion.10 = f32[256,512]{1,0:T(8,128)S(1)} fusion(f32[1024,512]{1,0:T(8,128)} %all-gather.5.cloned.1.call-done, s32[1024]{0:T(1024)S(1)} %pad_clamp_fusion.2), kind=kCustom, calls=%fused_computation.3.clone | custom fusion | bytes 1049600 | tf_op jit(solution)/shard_map/jit(_take)/gather | solution.py:55
  210.8 1.8 convolution_subtract_fusion.2
  212.8 11.7 %cholesky.164 = f32[128,128]{1,0:T(8,128)S(1)} custom-call(f32[128,128]{1,0:T(8,128)S(1)} %cholesky.197), custom_call_target="Cholesky" | custom-call | tf_op jit(solution)/shard_map/jit(cholesky)/cholesky | solution.py:91
  224.6 9.8 %custom-call.15 = f32[1,128,128]{1,2,0:T(8,128)S(1)} custom-call(f32[1,128,128]{2,1,0:T(8,128)S(1)} %get-tuple-element.75), custom_call_target="InvertDiagBlocksLowerTriangular" | custom-call | tf_op jit(solution)/shard_map/jit(cholesky)/cholesky | solution.py:91
  234.9 11.9 %cholesky.181 = f32[128,128]{1,0:T(8,128)S(1)} custom-call(f32[128,128]{1,0:T(8,128)S(1)} %convolution_subtract_fusion.5), custom_call_target="Cholesky" | custom-call | tf_op jit(solution)/shard_map/jit(cholesky)/cholesky | solution.py:91
  249.4 3.9 %while.5 = (s32[]{:T(128)}, f32[256,256]{1,0:T(8,128)S(1)}, s32[2,2]{1,0:T(2,128)S(1)}, f32[2,128,128]{2,1,0:T(8,128)S(1)}, s32[]{:T(128)}) while((s32[]{:T(128)}, f32[256,256]{1,0:T(8,128)S(1)}, s32[2,2]{1,0:T(2,128)S(1)}, f32[2,128,128]{2,1,0:T(8,128)S(1)}, s32[]{:T(128)}) %tuple.91), condition=%wide.while_cond.clone, body=%wide.while_body.clone.sunk | while | flops 2 | bytes 131181 | solution.py:92
  253.3 19.7 %custom-call.16 = f32[2,128,128]{1,2,0:T(8,128)S(1)} custom-call(f32[2,128,128]{2,1,0:T(8,128)S(1)} %get-tuple-element.23), custom_call_target="InvertDiagBlocksLowerTriangular" | custom-call | tf_op jit(solution)/shard_map/jit(_solve_triangular)/triangular_solve | solution.py:92
  273.0 2.1 fusion
  (184 shorter events, 35.2 us)
Async XLA Ops:
  8.0 64.3 %all-gather.3.cloned.1.call-start = ((), (), s32[]{:S(2)}) async-start(), calls=%async_computation.2 | async-start | bytes 1081344 | tf_op jit(solution)/shard_map/all_gather | solution.py:48
  9.6 55.4 %copy-start.9 = (s32[256]{0:T(256)}, s32[256]{0:T(256)S(1)}, u32[]{:S(2)}) copy-start(s32[256]{0:T(256)S(1)} %get-tuple-element.96) | copy-start | bytes 3076
  12.4 135.7 %reduce-scatter.3.cloned.1.call-start = ((), (), s32[]{:S(2)}) async-start(), calls=%async_computation.3 | async-start | bytes 1179648 | tf_op jit(solution)/shard_map/reduce_scatter | solution.py:62
  14.3 61.2 %copy-start.11 = (pred[256]{0:T(512)(128)(4,1)}, pred[256]{0:T(512)(128)(4,1)S(1)}, u32[]{:S(2)}) copy-start(pred[256]{0:T(512)(128)(4,1)S(1)} %get-tuple-element.58) | copy-start | bytes 772
  14.3 61.2 %copy-start.13 = (pred[256]{0:T(512)(128)(4,1)}, pred[256]{0:T(512)(128)(4,1)S(1)}, u32[]{:S(2)}) copy-start(pred[256]{0:T(512)(128)(4,1)S(1)} %get-tuple-element.80) | copy-start | bytes 772
  63.9 7.0 %copy-start.31 = (u32[32]{0:T(128)S(1)}, u32[32]{0:T(128)}, u32[]{:S(2)}) copy-start(u32[32]{0:T(128)} %constant.204) | copy-start | bytes 388
  63.9 142.9 %all-gather.5.cloned.1.call-start = ((), (), s32[]{:S(2)}) async-start(), calls=%async_computation.4 | async-start | bytes 2162688 | tf_op jit(solution)/shard_map/all_gather | solution.py:48
  64.2 8.1 %copy-start.20 = (f32[256]{0:T(256)}, f32[256]{0:T(256)S(1)}, u32[]{:S(2)}) copy-start(f32[256]{0:T(256)S(1)} %multiply_reduce_fusion.2) | copy-start | bytes 3076
  75.5 37.2 %copy-start.32 = (s32[2]{0:T(128)S(1)}, s32[2]{0:T(128)}, u32[]{:S(2)}) copy-start(s32[2]{0:T(128)} %iota_multiply_fusion) | copy-start | bytes 28
  76.1 72.1 %copy-start.12 = (pred[256]{0:T(512)(128)(4,1)S(1)}, pred[256]{0:T(512)(128)(4,1)}, u32[]{:S(2)}) copy-start(pred[256]{0:T(512)(128)(4,1)} %copy-done.11) | copy-start | bytes 772
  76.1 72.1 %copy-start.14 = (pred[256]{0:T(512)(128)(4,1)S(1)}, pred[256]{0:T(512)(128)(4,1)}, u32[]{:S(2)}) copy-start(pred[256]{0:T(512)(128)(4,1)} %copy-done.13) | copy-start | bytes 772
  76.1 72.1 %copy-start.21 = (f32[256]{0:T(256)S(1)}, f32[256]{0:T(256)}, u32[]{:S(2)}) copy-start(f32[256]{0:T(256)} %copy-done.20) | copy-start | bytes 3076
  128.4 21.8 %copy-start.29 = (s32[2,2]{1,0:T(2,128)}, s32[2,2]{1,0:T(2,128)S(1)}, u32[]{:S(2)}) copy-start(s32[2,2]{1,0:T(2,128)S(1)} %get-tuple-element.204) | copy-start | bytes 52
  153.6 119.4 %reduce-scatter.5.cloned.1.call-start = ((), (), s32[]{:S(2)}) async-start(), calls=%async_computation.5 | async-start | bytes 1179648 | tf_op jit(solution)/shard_map/reduce_scatter | solution.py:62
  154.3 42.2 %copy-start.16 = (pred[256]{0:T(512)(128)(4,1)}, pred[256]{0:T(512)(128)(4,1)S(1)}, u32[]{:S(2)}) copy-start(pred[256]{0:T(512)(128)(4,1)S(1)} %get-tuple-element.62) | copy-start | bytes 772
  154.4 42.3 %copy-start.18 = (pred[256]{0:T(512)(128)(4,1)}, pred[256]{0:T(512)(128)(4,1)S(1)}, u32[]{:S(2)}) copy-start(pred[256]{0:T(512)(128)(4,1)S(1)} %get-tuple-element.90) | copy-start | bytes 772
  198.2 8.6 %copy-start.22 = (f32[256]{0:T(256)}, f32[256]{0:T(256)S(1)}, u32[]{:S(2)}) copy-start(f32[256]{0:T(256)S(1)} %multiply_reduce_fusion.1) | copy-start | bytes 3076
  206.9 3.0 %copy-start = (f32[1024,512]{1,0:T(8,128)S(1)}, f32[1024,512]{1,0:T(8,128)}, u32[]{:S(2)}) copy-start(f32[1024,512]{1,0:T(8,128)} %all-gather.5.cloned.1.call-done) | copy-start | bytes 6291460
  210.8 38.6 %copy-start.30 = (s32[2,2]{1,0:T(2,128)S(1)}, s32[2,2]{1,0:T(2,128)}, u32[]{:S(2)}) copy-start(s32[2,2]{1,0:T(2,128)} %copy-done.29) | copy-start | bytes 52
  212.6 60.4 %copy-start.4 = (f32[384,256]{0,1:T(8,128)S(1)}, f32[384,256]{0,1:T(8,128)}, u32[]{:S(2)}) copy-start(f32[384,256]{0,1:T(8,128)} %copy-done.3) | copy-start | bytes 1179652
  212.6 60.4 %copy-start.17 = (pred[256]{0:T(512)(128)(4,1)S(1)}, pred[256]{0:T(512)(128)(4,1)}, u32[]{:S(2)}) copy-start(pred[256]{0:T(512)(128)(4,1)} %copy-done.16) | copy-start | bytes 772
  212.6 60.4 %copy-start.19 = (pred[256]{0:T(512)(128)(4,1)S(1)}, pred[256]{0:T(512)(128)(4,1)}, u32[]{:S(2)}) copy-start(pred[256]{0:T(512)(128)(4,1)} %copy-done.18) | copy-start | bytes 772
  212.6 60.4 %copy-start.23 = (f32[256]{0:T(256)S(1)}, f32[256]{0:T(256)}, u32[]{:S(2)}) copy-start(f32[256]{0:T(256)} %copy-done.22) | copy-start | bytes 3076
  273.0 3.4 %copy-start.6 = (f32[1,384,256]{1,2,0:T(8,128)S(1)}, f32[1,384,256]{1,2,0:T(8,128)}, u32[]{:S(2)}) copy-start(f32[1,384,256]{1,2,0:T(8,128)} %get-tuple-element.70) | copy-start | bytes 1179652
  (13 other events, 26.4 us)
Sparse Core Ops, SparseCore 0:
  12.6 57.0 all-gather.2
  153.7 53.1 all-gather.4
Sparse Core Ops, SparseCore 1:
  64.0 4.2 reduce-scatter.2
  198.2 5.6 reduce-scatter.4
where the time goes:
time: 290 us; the launch traced here: 286 us
  other arithmetic  119 us (41%)
  blocking collectives  88.1 us (30%)
  local copies, waits for them, and re-layouts  27.1 us (9%)
  between operations  19.7 us (7%)
  matrix products  13.1 us (5%)
  loops' own time  11.6 us (4%)
  waiting for transfers between devices  7.08 us (2%)
    all_gather x2, blocking collectives, shards(): all_x = lax.all_gather(packed_x, ('rows', 'feat'), axis=0, tiled=True)  85.3 us
    another operation x14, other arithmetic, shards(): chol_lower = jnp.linalg.cholesky(pivot_block)  69.4 us
    another operation x5, other arithmetic, shards(): jax.scipy.linalg.solve_triangular(chol_lower, kernel_panel.T, lower=True)  39.9 us
    another operation x2, loops' own time, shards(): jax.scipy.linalg.solve_triangular(chol_lower, kernel_panel.T, lower=True)  11.6 us
    another operation x15, local copies, waits for them, and re-layouts, shards(): jax.scipy.linalg.solve_triangular(chol_lower, kernel_panel.T, lower=True)  7.88 us
    gather x4, local copies, waits for them, and re-layouts, shards(): pivot_factor = pivot_factor + jnp.take(all_f, source, axis=0)  7.17 us
    all_gather x2, waiting for transfers between devices, shards(): all_f = lax.all_gather(packed_f, ('rows', 'feat'), axis=0, tiled=True)  6.96 us
  transfers between devices with their start and end apart: 4, of which 1 were waited for; matrix products, arithmetic and copies ran while one was open for 50% of the time, Pallas kernels for 0%

commit v1 on v0

--- a/solution.py
+++ b/solution.py
@@ -44,7 +44,24 @@
         slot_half_rows = jnp.sum(jnp.where(half_hits, half_safe[None, :], 0), axis=1)
         packed_x = jnp.where(slot_full[:, None], jnp.take(embeddings, slot_rows, axis=0), 0)
         packed_f = jnp.where(slot_half[:, None], jnp.take(current, slot_half_rows, axis=0), 0.0)
-        all_x = lax.all_gather(packed_x, ("rows", "feat"), axis=0, tiled=True)
+        ways, here, lap = (
+            lax.axis_size(("rows", "feat")),
+            lax.axis_index(("rows", "feat")),
+            packed_x.shape[0],
+        )
+        line, have = (packed_x, 1)
+        while have < ways:
+            line = jnp.concatenate(
+                [
+                    line,
+                    lax.ppermute(
+                        line, ("rows", "feat"), [(d, (d - have) % ways) for d in range(ways)]
+                    ),
+                ],
+                axis=0,
+            )
+            have = 2 * have
+        all_x = jnp.roll(line, here * lap, axis=0)
         all_f = lax.all_gather(packed_f, ("rows", "feat"), axis=0, tiled=True)
         first_src = owners * feat_count * capacity + pivot_ranks
         pieces = []

time: 290 us -> 314 us (1.083)
  waiting for transfers between devices: 7.08 us -> 100 us
  blocking collectives: 88.1 us -> 2.47 us
  starting transfers between devices: 0.17 us -> 16.8 us
  loops' own time: 11.6 us -> 0.1 us
  local copies, waits for them, and re-layouts: 27.1 us -> 35 us
    all_gather x2 -> x0, blocking collectives: 85.3 us -> none  [shards(): all_x = lax.all_gather(packed_x, ('rows', 'feat'), axis=0, tiled=True)]
    ppermute x0 -> x10, waiting for transfers between devices: none -> 46.7 us  [shards(): lax.ppermute(line, ('rows', 'feat'), [(d, (d - have) % ways) for d in ran...]
    all_gather x2, waiting for transfers between devices: 6.96 us -> 53.1 us  [shards(): all_f = lax.all_gather(packed_f, ('rows', 'feat'), axis=0, tiled=True)]
    ppermute x0 -> x10, starting transfers between devices: none -> 16 us  [shards(): lax.ppermute(line, ('rows', 'feat'), [(d, (d - have) % ways) for d in ran...]
    another operation x2, loops' own time: 11.6 us -> 0.1 us  [shards(): jax.scipy.linalg.solve_triangular(chol_lower, kernel_panel.T, lower=True)]
  transfers between devices with their start and end apart: 4 -> 14, of which waited for: 1 -> 7; matrix products, arithmetic and copies ran while one was open for 50% -> 49% of each run, Pallas kernels for 0% -> 0%
where the time goes in v1:
time: 314 us; the launch traced here: 308 us
  other arithmetic  120 us (38%)
  waiting for transfers between devices  100 us (32%)
  local copies, waits for them, and re-layouts  35 us (11%)
  between operations  19.7 us (6%)
  starting transfers between devices  16.8 us (5%)
  matrix products  14.8 us (5%)
    another operation x14, other arithmetic, shards(): chol_lower = jnp.linalg.cholesky(pivot_block)  69.4 us
    all_gather x2, waiting for transfers between devices, shards(): all_f = lax.all_gather(packed_f, ('rows', 'feat'), axis=0, tiled=True)  53.1 us
    ppermute x10, waiting for transfers between devices, shards(): lax.ppermute(line, ('rows', 'feat'), [(d, (d - have) % ways) for d in ran...  46.7 us
    another operation x5, other arithmetic, shards(): jax.scipy.linalg.solve_triangular(chol_lower, kernel_panel.T, lower=True)  39.4 us
    ppermute x10, starting transfers between devices, shards(): lax.ppermute(line, ('rows', 'feat'), [(d, (d - have) % ways) for d in ran...  16 us
    gather x4, local copies, waits for them, and re-layouts, shards(): pivot_factor = pivot_factor + jnp.take(all_f, source, axis=0)  7.99 us
    another operation x15, local copies, waits for them, and re-layouts, shards(): jax.scipy.linalg.solve_triangular(chol_lower, kernel_panel.T, lower=True)  7.66 us
  transfers between devices with their start and end apart: 14, of which 7 were waited for; matrix products, arithmetic and copies ran while one was open for 49% of the time, Pallas kernels for 0%

profile of v1, /device:TPU:0, one launch (start us, length us, event | category | flops | bytes accessed | tf_op | source)
XLA Modules:
  0.0 308.4 jit_solution(13876025045779841711)
XLA Ops:
  12.8 1.8 gather_fusion.2
  14.7 6.5 %collective-permute-start = (bf16[32,384]{1,0:T(8,128)(2,1)S(1)}, bf16[32,384]{1,0:T(8,128)(2,1)S(1)}, u32[]{:S(2)}, u32[]{:S(2)}) collective-permute-start(bf16[32,384]{1,0:T(8,128)(2,1)S(1)} %get-tuple-element.64), channel_id=1, source_target_pairs={{0,31},{1,0},{2,1},{3,2},{4,3},{5,4},{6,5},{7,6},{8,7},{9,8},{10,9... | collective-permute-start | bytes 73736 | tf_op jit(solution)/shard_map/ppermute | solution.py:57
  21.3 1.8 gather_fusion.7
  32.9 2.1 collective-permute-done.2
  38.2 9.1 %collective-permute-done.8 = bf16[256,384]{1,0:T(8,128)(2,1)S(1)} collective-permute-done((bf16[256,384]{1,0:T(8,128)(2,1)S(1)}, bf16[256,384]{1,0:T(8,128)(2,1)S(1)}, u32[]{:S(2)}, u32[]{:S(2)}) %collective-permute-start.8) | collective-permute-done | bytes 196640 | tf_op jit(solution)/shard_map/ppermute | solution.py:57
  48.2 2.9 collective-permute-start.4
  52.5 2.5 all-reduce.1
  55.1 22.9 %collective-permute-done.9 = bf16[512,384]{1,0:T(8,128)(2,1)S(1)} collective-permute-done((bf16[512,384]{1,0:T(8,128)(2,1)S(1)}, bf16[512,384]{1,0:T(8,128)(2,1)S(1)}, u32[]{:S(2)}, u32[]{:S(2)}) %collective-permute-start.9) | collective-permute-done | bytes 393248 | tf_op jit(solution)/shard_map/ppermute | solution.py:57
  78.1 10.2 %collective-permute-done.4 = bf16[512,384]{1,0:T(8,128)(2,1)S(1)} collective-permute-done((bf16[512,384]{1,0:T(8,128)(2,1)S(1)}, bf16[512,384]{1,0:T(8,128)(2,1)S(1)}, u32[]{:S(2)}, u32[]{:S(2)}) %collective-permute-start.4) | collective-permute-done | bytes 393248 | tf_op jit(solution)/shard_map/ppermute | solution.py:57
  89.2 2.3 fusion.13
  97.0 2.3 gather_fusion.6
  102.8 11.7 %cholesky.130 = f32[128,128]{1,0:T(8,128)S(1)} custom-call(f32[128,128]{1,0:T(8,128)S(1)} %cholesky.194), custom_call_target="Cholesky" | custom-call | tf_op jit(solution)/shard_map/jit(cholesky)/cholesky | solution.py:108
  114.6 9.8 %custom-call.13 = f32[1,128,128]{1,2,0:T(8,128)S(1)} custom-call(f32[1,128,128]{2,1,0:T(8,128)S(1)} %get-tuple-element.92), custom_call_target="InvertDiagBlocksLowerTriangular" | custom-call | tf_op jit(solution)/shard_map/jit(cholesky)/cholesky | solution.py:108
  124.9 11.7 %cholesky.147 = f32[128,128]{1,0:T(8,128)S(1)} custom-call(f32[128,128]{1,0:T(8,128)S(1)} %convolution_subtract_fusion.6), custom_call_target="Cholesky" | custom-call | tf_op jit(solution)/shard_map/jit(cholesky)/cholesky | solution.py:108
  139.3 4.0 %while.4 = (s32[]{:T(128)}, f32[256,256]{1,0:T(8,128)S(1)}, s32[2,2]{1,0:T(2,128)S(1)}, f32[2,128,128]{2,1,0:T(8,128)S(1)}, s32[]{:T(128)}) while((s32[]{:T(128)}, f32[256,256]{1,0:T(8,128)S(1)}, s32[2,2]{1,0:T(2,128)S(1)}, f32[2,128,128]{2,1,0:T(8,128)S(1)}, s32[]{:T(128)}) %tuple.92), condition=%wide.while_cond, body=%wide.while_body.sunk | while | flops 2 | bytes 131189 | solution.py:109
  143.3 19.7 %custom-call.14 = f32[2,128,128]{1,2,0:T(8,128)S(1)} custom-call(f32[2,128,128]{2,1,0:T(8,128)S(1)} %get-tuple-element.23), custom_call_target="InvertDiagBlocksLowerTriangular" | custom-call | tf_op jit(solution)/shard_map/jit(_solve_triangular)/triangular_solve | solution.py:109
  176.4 53.1 %all-gather.5.cloned.1.call-done = f32[1024,512]{1,0:T(8,128)} async-done(((f32[32,512]{1,0:T(8,128)}), f32[1024,512]{1,0:T(8,128)}) %all-gather.5.cloned.1.call-update) | async-done | bytes 2097168 | tf_op jit(solution)/shard_map/all_gather | solution.py:65
  229.5 3.1 %gather_fusion.11 = f32[256,512]{1,0:T(8,128)S(1)} fusion(f32[1024,512]{1,0:T(8,128)} %all-gather.5.cloned.1.call-done, s32[1024]{0:T(1024)} %copy-done.9), kind=kCustom, calls=%fused_computation.9.clone | custom fusion | bytes 1049600 | tf_op jit(solution)/shard_map/jit(_take)/gather | solution.py:72
  235.5 11.7 %cholesky.164 = f32[128,128]{1,0:T(8,128)S(1)} custom-call(f32[128,128]{1,0:T(8,128)S(1)} %cholesky.197), custom_call_target="Cholesky" | custom-call | tf_op jit(solution)/shard_map/jit(cholesky)/cholesky | solution.py:108
  247.3 9.8 %custom-call.15 = f32[1,128,128]{1,2,0:T(8,128)S(1)} custom-call(f32[1,128,128]{2,1,0:T(8,128)S(1)} %get-tuple-element.88), custom_call_target="InvertDiagBlocksLowerTriangular" | custom-call | tf_op jit(solution)/shard_map/jit(cholesky)/cholesky | solution.py:108
  257.6 11.9 %cholesky.181 = f32[128,128]{1,0:T(8,128)S(1)} custom-call(f32[128,128]{1,0:T(8,128)S(1)} %convolution_subtract_fusion.5), custom_call_target="Cholesky" | custom-call | tf_op jit(solution)/shard_map/jit(cholesky)/cholesky | solution.py:108
  272.1 3.7 %while.5 = (s32[]{:T(128)}, f32[256,256]{1,0:T(8,128)S(1)}, s32[2,2]{1,0:T(2,128)S(1)}, f32[2,128,128]{2,1,0:T(8,128)S(1)}, s32[]{:T(128)}) while((s32[]{:T(128)}, f32[256,256]{1,0:T(8,128)S(1)}, s32[2,2]{1,0:T(2,128)S(1)}, f32[2,128,128]{2,1,0:T(8,128)S(1)}, s32[]{:T(128)}) %tuple.106), condition=%wide.while_cond.clone, body=%wide.while_body.clone.sunk | while | flops 2 | bytes 131189 | solution.py:109
  275.8 19.7 %custom-call.16 = f32[2,128,128]{1,2,0:T(8,128)S(1)} custom-call(f32[2,128,128]{2,1,0:T(8,128)S(1)} %get-tuple-element.24), custom_call_target="InvertDiagBlocksLowerTriangular" | custom-call | tf_op jit(solution)/shard_map/jit(_solve_triangular)/triangular_solve | solution.py:109
  295.6 2.1 fusion
  (194 shorter events, 60.0 us)
Async XLA Ops:
  8.0 89.0 %all-gather.3.cloned.1.call-start = ((), (), s32[]{:S(2)}) async-start(), calls=%async_computation.2 | async-start | bytes 1081344 | tf_op jit(solution)/shard_map/all_gather | solution.py:65
  12.8 150.3 %reduce-scatter.3.cloned.1.call-start = ((), (), s32[]{:S(2)}) async-start(), calls=%async_computation.3 | async-start | bytes 1179648 | tf_op jit(solution)/shard_map/reduce_scatter | solution.py:79
  14.7 11.1 %collective-permute-start = (bf16[32,384]{1,0:T(8,128)(2,1)S(1)}, bf16[32,384]{1,0:T(8,128)(2,1)S(1)}, u32[]{:S(2)}, u32[]{:S(2)}) collective-permute-start(bf16[32,384]{1,0:T(8,128)(2,1)S(1)} %get-tuple-element.64), channel_id=1, source_target_pairs={{0,31},{1,0},{2,1},{3,2},{4,3},{5,4},{6,5},{7,6},{8,7},{9,8},{10,9... | collective-permute-start | bytes 73736 | tf_op jit(solution)/shard_map/ppermute | solution.py:57
  23.2 3.2 %collective-permute-start.5 = (bf16[32,384]{1,0:T(8,128)(2,1)S(1)}, bf16[32,384]{1,0:T(8,128)(2,1)S(1)}, u32[]{:S(2)}, u32[]{:S(2)}) collective-permute-start(bf16[32,384]{1,0:T(8,128)(2,1)S(1)} %get-tuple-element.70), channel_id=1, source_target_pairs={{0,31},{1,0},{2,1},{3,2},{4,3},{5,4},{6,5},{7,6},{8,7},{9,8},{10,9... | collective-permute-start | bytes 73736 | tf_op jit(solution)/shard_map/ppermute | solution.py:57
  25.8 4.1 %collective-permute-start.1 = (bf16[64,384]{1,0:T(8,128)(2,1)S(1)}, bf16[64,384]{1,0:T(8,128)(2,1)S(1)}, u32[]{:S(2)}, u32[]{:S(2)}) collective-permute-start(bf16[64,384]{1,0:T(8,128)(2,1)S(1)} %pad_maximum_fusion.12), channel_id=1, source_target_pairs={{0,30},{1,31},{2,0},{3,1},{4,2},{5,3},{6,4},{7,5},{8,6},{9,7},{10,... | collective-permute-start | bytes 147464 | tf_op jit(solution)/shard_map/ppermute | solution.py:57
  26.4 4.5 %collective-permute-start.6 = (bf16[64,384]{1,0:T(8,128)(2,1)S(1)}, bf16[64,384]{1,0:T(8,128)(2,1)S(1)}, u32[]{:S(2)}, u32[]{:S(2)}) collective-permute-start(bf16[64,384]{1,0:T(8,128)(2,1)S(1)} %pad_maximum_fusion.13), channel_id=1, source_target_pairs={{0,30},{1,31},{2,0},{3,1},{4,2},{5,3},{6,4},{7,5},{8,6},{9,7},{10,... | collective-permute-start | bytes 147464 | tf_op jit(solution)/shard_map/ppermute | solution.py:57
  30.0 21.1 %copy-start.5 = (f32[384,256]{1,0:T(8,128)S(1)}, f32[384,256]{1,0:T(8,128)}, u32[]{:S(2)}) copy-start(f32[384,256]{1,0:T(8,128)} %param.18) | copy-start | bytes 1179652
  30.0 5.0 %collective-permute-start.2 = (bf16[128,384]{1,0:T(8,128)(2,1)S(1)}, bf16[128,384]{1,0:T(8,128)(2,1)S(1)}, u32[]{:S(2)}, u32[]{:S(2)}) collective-permute-start(bf16[128,384]{1,0:T(8,128)(2,1)S(1)} %pad_maximum_fusion.10), channel_id=1, source_target_pairs={{0,28},{1,29},{2,30},{3,31},{4,0},{5,1},{6,2},{7,3},{8,4},{9,5},{1... | collective-permute-start | bytes 294920 | tf_op jit(solution)/shard_map/ppermute | solution.py:57
  31.0 6.1 %collective-permute-start.7 = (bf16[128,384]{1,0:T(8,128)(2,1)S(1)}, bf16[128,384]{1,0:T(8,128)(2,1)S(1)}, u32[]{:S(2)}, u32[]{:S(2)}) collective-permute-start(bf16[128,384]{1,0:T(8,128)(2,1)S(1)} %pad_maximum_fusion.11), channel_id=1, source_target_pairs={{0,28},{1,29},{2,30},{3,31},{4,0},{5,1},{6,2},{7,3},{8,4},{9,5},{1... | collective-permute-start | bytes 294920 | tf_op jit(solution)/shard_map/ppermute | solution.py:57
  35.0 16.3 %copy-start.20 = (u32[32]{0:T(128)S(1)}, u32[32]{0:T(128)}, u32[]{:S(2)}) copy-start(u32[32]{0:T(128)} %constant.224) | copy-start | bytes 388
  35.0 12.4 %collective-permute-start.3 = (bf16[256,384]{1,0:T(8,128)(2,1)S(1)}, bf16[256,384]{1,0:T(8,128)(2,1)S(1)}, u32[]{:S(2)}, u32[]{:S(2)}) collective-permute-start(bf16[256,384]{1,0:T(8,128)(2,1)S(1)} %pad_maximum_fusion.8), channel_id=1, source_target_pairs={{0,24},{1,25},{2,26},{3,27},{4,28},{5,29},{6,30},{7,31},{8,0},{9,1... | collective-permute-start | bytes 589832 | tf_op jit(solution)/shard_map/ppermute | solution.py:57
  37.1 10.2 %collective-permute-start.8 = (bf16[256,384]{1,0:T(8,128)(2,1)S(1)}, bf16[256,384]{1,0:T(8,128)(2,1)S(1)}, u32[]{:S(2)}, u32[]{:S(2)}) collective-permute-start(bf16[256,384]{1,0:T(8,128)(2,1)S(1)} %pad_maximum_fusion.9), channel_id=1, source_target_pairs={{0,24},{1,25},{2,26},{3,27},{4,28},{5,29},{6,30},{7,31},{8,0},{9,1... | collective-permute-start | bytes 589832 | tf_op jit(solution)/shard_map/ppermute | solution.py:57
  47.4 30.6 %collective-permute-start.9 = (bf16[512,384]{1,0:T(8,128)(2,1)S(1)}, bf16[512,384]{1,0:T(8,128)(2,1)S(1)}, u32[]{:S(2)}, u32[]{:S(2)}) collective-permute-start(bf16[512,384]{1,0:T(8,128)(2,1)S(1)} %get-tuple-element.79), channel_id=1, source_target_pairs={{0,16},{1,17},{2,18},{3,19},{4,20},{5,21},{6,22},{7,23},{8,24},{9,... | collective-permute-start | bytes 1179656 | tf_op jit(solution)/shard_map/ppermute | solution.py:57
  48.2 40.1 %collective-permute-start.4 = (bf16[512,384]{1,0:T(8,128)(2,1)S(1)}, bf16[512,384]{1,0:T(8,128)(2,1)S(1)}, u32[]{:S(2)}, u32[]{:S(2)}) collective-permute-start(bf16[512,384]{1,0:T(8,128)(2,1)S(1)} %get-tuple-element.77), channel_id=1, source_target_pairs={{0,16},{1,17},{2,18},{3,19},{4,20},{5,21},{6,22},{7,23},{8,24},{9,... | collective-permute-start | bytes 1179656 | tf_op jit(solution)/shard_map/ppermute | solution.py:57
  78.1 10.3 %copy-start.8 = (bf16[1024,384]{1,0:T(8,128)(2,1)}, bf16[1024,384]{1,0:T(8,128)(2,1)S(1)}, u32[]{:S(2)}) copy-start(bf16[1024,384]{1,0:T(8,128)(2,1)S(1)} %constant_dynamic-update-slice_fusion.16) | copy-start | bytes 2359300
  96.5 133.0 %all-gather.5.cloned.1.call-start = ((), (), s32[]{:S(2)}) async-start(), calls=%async_computation.4 | async-start | bytes 2162688 | tf_op jit(solution)/shard_map/all_gather | solution.py:65
  102.8 60.3 %copy-start.6 = (f32[256,256]{1,0:T(8,128)S(1)}, f32[256,256]{1,0:T(8,128)}, u32[]{:S(2)}) copy-start(f32[256,256]{1,0:T(8,128)} %gather_fusion.5) | copy-start | bytes 786436
  143.3 22.5 %copy-start.18 = (s32[2,2]{1,0:T(2,128)}, s32[2,2]{1,0:T(2,128)S(1)}, u32[]{:S(2)}) copy-start(s32[2,2]{1,0:T(2,128)S(1)} %get-tuple-element.253) | copy-start | bytes 52
  170.3 125.2 %reduce-scatter.5.cloned.1.call-start = ((), (), s32[]{:S(2)}) async-start(), calls=%async_computation.5 | async-start | bytes 1179648 | tf_op jit(solution)/shard_map/reduce_scatter | solution.py:79
  235.3 36.8 %copy-start.19 = (s32[2,2]{1,0:T(2,128)S(1)}, s32[2,2]{1,0:T(2,128)}, u32[]{:S(2)}) copy-start(s32[2,2]{1,0:T(2,128)} %copy-done.18) | copy-start | bytes 52
  235.5 60.1 %copy-start.4 = (f32[384,256]{0,1:T(8,128)S(1)}, f32[384,256]{0,1:T(8,128)}, u32[]{:S(2)}) copy-start(f32[384,256]{0,1:T(8,128)} %copy-done.3) | copy-start | bytes 1179652
  235.5 60.1 %copy-start.12 = (pred[256]{0:T(512)(128)(4,1)S(1)}, pred[256]{0:T(512)(128)(4,1)}, u32[]{:S(2)}) copy-start(pred[256]{0:T(512)(128)(4,1)} %copy-done.11) | copy-start | bytes 772
  235.5 60.1 %copy-start.14 = (pred[256]{0:T(512)(128)(4,1)S(1)}, pred[256]{0:T(512)(128)(4,1)}, u32[]{:S(2)}) copy-start(pred[256]{0:T(512)(128)(4,1)} %copy-done.13) | copy-start | bytes 772
  235.5 60.1 %copy-start.16 = (f32[256]{0:T(256)S(1)}, f32[256]{0:T(256)}, u32[]{:S(2)}) copy-start(f32[256]{0:T(256)} %copy-done.15) | copy-start | bytes 3076
  (11 other events, 21.2 us)
Sparse Core Ops, SparseCore 0:
  12.9 77.3 all-gather.2
  170.5 58.9 all-gather.4
Sparse Core Ops, SparseCore 1:
  96.6 10.9 reduce-scatter.2
  175.8 10.9 reduce-scatter.4
